TPU v7x, 256 devices: a whole 4x4x8 slice. The times are simulated.
256 devices in a mesh: mp: 2 (over x_hi), row: 8 (over z), col: 16 (over x_lo, y, core).
Axes of the slice: x: 4 (x_hi: 2, x_lo: 2; x = x_hi * 2 + x_lo), y: 4, z: 8, core: 2. Of those that a mesh axis runs over, the one named last changes fastest.
Arguments:
- gram_tiles: bfloat16 [4, 16, 8, 128, 16384], P('mp', None, 'row', None, 'col'), may hold values from -4 to 64, as said below
- weights: bfloat16 [4, 16384, 128], P('mp', ('col', 'row')), may hold values from -8 to 8
- damping: float32 [128], replicated, may hold values from 0.5 to 4
Outputs:
- merged: float32 [16384, 128], P(('col', 'row'))
- residual: float32 [16384, 128], P(('col', 'row'))
Inputs may be any that keep to these rules, and one draw needn't show every extreme that they name: `gram_tiles`: each model's 16384 x 16384 Gram, read as in the first step, is symmetric positive definite.
All inputs are finite; a program needn't handle non-finite values.
Results may differ from a plain program's by a relative error of at most 0.012.
The roundings to bfloat16 on the way count: a program that leaves them out, or rounds other values in their place, can miss the bound.
Values may be sent and summed in bfloat16 or wider, within the bound.
No kernel may reach another device: no remote copies, remote signals or barrier semaphores. Data moves between devices by JAX's collectives and lax.ppermute only.
A program may use at most 64 MiB of HBM per device.

v0:
```python
import jax
import jax.numpy as jnp
from jax import lax
from jax.sharding import PartitionSpec as P

ITERS = 2


def contract_rows(gram_tile, portion):
    spread = jnp.broadcast_to(portion, (gram_tile.shape[0],) + portion.shape[1:])
    return jnp.einsum("mij,mjk->ik", gram_tile, spread, preferred_element_type=jnp.float32)


def apply_models(gram_tile, vectors):
    partial_value = contract_rows(gram_tile, lax.all_gather(vectors, "row", axis=1, tiled=True))
    summed = lax.psum_scatter(partial_value, "col", scatter_dimension=0, tiled=True)
    return (lax.psum(summed, "mp"), partial_value)


def squares(residual):
    return lax.psum(jnp.sum(residual * residual, axis=0), ("row", "col"))


def on_device(gram_tiles, weights, damping):
    shape_in = gram_tiles.shape
    gram_tile = gram_tiles.reshape(
        shape_in[0], shape_in[1] * shape_in[2] * shape_in[3], shape_in[4]
    )
    target, unused = apply_models(gram_tile, weights)
    merged = jnp.zeros_like(target)
    residual = target
    direction = target
    norm_now = squares(residual)
    for iteration in range(ITERS):
        low_dir = direction.astype(jnp.bfloat16)
        applied, partial_value = apply_models(gram_tile, low_dir[None])
        dir_wide = low_dir.astype(jnp.float32)
        applied = applied + damping[None, :] * dir_wide
        curve_term = lax.psum(jnp.sum(dir_wide * applied, axis=0), ("row", "col"))
        step_size = norm_now / curve_term
        merged = merged + step_size[None, :] * direction
        residual = residual - step_size[None, :] * applied
        if iteration + 1 < ITERS:
            norm_next = squares(residual)
            direction = residual + (norm_next / norm_now)[None, :] * direction
            norm_now = norm_next
    return (merged, residual)


def solution(mesh):
    in_specs = (P("mp", None, "row", None, "col"), P("mp", ("col", "row"), None), P())
    out_specs = (P(("col", "row"), None), P(("col", "row"), None))
    return jax.shard_map(
        on_device, mesh=mesh, in_specs=in_specs, out_specs=out_specs, check_vma=False
    )
```

profile of v0, /device:TPU:4, one launch (start us, length us, event | category | flops | bytes accessed | tf_op | source)
XLA Modules:
  0.0 1248.6 jit_solution(5157626509282699537)
XLA Ops:
  7.2 29.3 %all_gather.9 = bf16[2,1024,128]{2,1,0:T(8,128)(2,1)S(1)} all-gather(bf16[2,128,128]{2,1,0:T(8,128)(2,1)} %param.4), channel_id=1, replica_groups=mesh['mp'=2,'row'=8,'col'=16] {'row'}, dimensions={1}, use_global_device_ids=true | all-gather | bytes 589824 | tf_op jit(solution)/shard_map/all_gather | solution.py:15
  36.5 6.7 convolution_bitcast_fusion.2
  43.3 63.9 %reduce-scatter.4.cloned.1.call-done = f32[128,128]{1,0:T(8,128)} async-done(((f32[2048,128]{1,0:T(8,128)}), f32[128,128]{1,0:T(8,128)}) %reduce-scatter.4.cloned.1.call-update) | async-done | bytes 65552 | tf_op jit(solution)/shard_map/reduce_scatter | solution.py:16
  107.3 33.3 %all-reduce.5.cloned.1.call-done = f32[128,128]{1,0:T(8,128)} async-done(((f32[128,128]{1,0:T(8,128)}), f32[128,128]{1,0:T(8,128)}) %all-reduce.5.cloned.1.call-update) | async-done | bytes 65552 | tf_op jit(solution)/shard_map/psum | solution.py:17
  140.6 0.9 convert_element_type.12
  141.5 26.0 %all-gather = bf16[1024,128]{1,0:T(8,128)(2,1)S(1)} all-gather(bf16[128,128]{1,0:T(8,128)(2,1)S(1)} %convert_element_type.12), channel_id=2, replica_groups=mesh['mp'=2,'row'=8,'col'=16] {'row'}, dimensions={0}, use_global_device_ids=true | all-gather | bytes 294912 | tf_op jit(solution)/shard_map/all_gather | solution.py:15
  167.6 0.1 copy.5
  167.7 6.7 convolution_bitcast_fusion.1
  174.5 65.0 %reduce-scatter.6.cloned.1.call-done = f32[128,128]{1,0:T(8,128)} async-done(((f32[2048,128]{1,0:T(8,128)}), f32[128,128]{1,0:T(8,128)}) %reduce-scatter.6.cloned.1.call-update) | async-done | bytes 65552 | tf_op jit(solution)/shard_map/reduce_scatter | solution.py:16
  239.6 33.3 %all-reduce.7.cloned.1.call-done = f32[128,128]{1,0:T(8,128)} async-done(((f32[128,128]{1,0:T(8,128)}), f32[128,128]{1,0:T(8,128)}) %all-reduce.7.cloned.1.call-update) | async-done | bytes 65552 | tf_op jit(solution)/shard_map/psum | solution.py:17
  272.9 0.9 fusion.3
  273.8 281.3 %all-reduce = (f32[128]{0:T(128)S(1)}, f32[128]{0:T(128)S(1)}) all-reduce(f32[128]{0:T(128)S(1)} %get-tuple-element.3, f32[128]{0:T(128)S(1)} %get-tuple-element.2), channel_id=1, replica_groups=mesh['mp'=2,'row'=8,'col'=16] {'row','col'}, use_global_device_ids=true, to_apply=%region_3.0 | all-reduce | flops 256 | bytes 2048 | tf_op jit(solution)/shard_map/psum | solution.py:21
  555.1 0.9 multiply_reduce_fusion
  556.0 275.6 %psum.53 = f32[128]{0:T(128)S(1)} all-reduce(f32[128]{0:T(128)S(1)} %multiply_reduce_fusion), channel_id=1, replica_groups=mesh['mp'=2,'row'=8,'col'=16] {'row','col'}, use_global_device_ids=true, to_apply=%region_9.0 | all-reduce | flops 128 | bytes 1024 | tf_op jit(solution)/shard_map/psum | solution.py:21
  831.6 0.9 fusion.6
  832.4 24.9 %all-gather.1 = bf16[1024,128]{1,0:T(8,128)(2,1)S(1)} all-gather(bf16[128,128]{1,0:T(8,128)(2,1)S(1)} %fusion.6), channel_id=3, replica_groups=mesh['mp'=2,'row'=8,'col'=16] {'row'}, dimensions={0}, use_global_device_ids=true | all-gather | bytes 294912 | tf_op jit(solution)/shard_map/all_gather | solution.py:15
  857.3 0.1 copy.7
  857.5 6.7 convolution_bitcast_fusion
  864.2 0.0 all-reduce.9.cloned.1.call-start
  864.3 60.5 %reduce-scatter.8.cloned.1.call-done = f32[128,128]{1,0:T(8,128)} async-done(((f32[2048,128]{1,0:T(8,128)}), f32[128,128]{1,0:T(8,128)}) %reduce-scatter.8.cloned.1.call-update) | async-done | bytes 65552 | tf_op jit(solution)/shard_map/reduce_scatter | solution.py:16
  924.8 33.2 %all-reduce.9.cloned.1.call-done = f32[128,128]{1,0:T(8,128)} async-done(((f32[128,128]{1,0:T(8,128)}), f32[128,128]{1,0:T(8,128)}) %all-reduce.9.cloned.1.call-update) | async-done | bytes 65552 | tf_op jit(solution)/shard_map/psum | solution.py:17
  958.1 0.9 fusion.5
  958.9 281.3 %psum.55 = f32[128]{0:T(128)S(1)} all-reduce(f32[128]{0:T(128)S(1)} %fusion.5), channel_id=1, replica_groups=mesh['mp'=2,'row'=8,'col'=16] {'row','col'}, use_global_device_ids=true, to_apply=%region_13.0 | all-reduce | flops 128 | bytes 1024 | tf_op jit(solution)/shard_map/psum | solution.py:39
  1240.2 1.5 multiply_subtract_fusion
  (20 shorter events, 0.3 us)
Async XLA Ops:
  7.2 100.1 %reduce-scatter.4.cloned.1.call-start = ((), (), s32[]{:S(2)}) async-start(), calls=%async_computation.3 | async-start | bytes 1114112 | tf_op jit(solution)/shard_map/reduce_scatter | solution.py:16
  43.3 229.6 %copy-start.2 = (f32[128]{0:T(128)S(1)}, f32[128]{0:T(128)}, u32[]{:S(2)}) copy-start(f32[128]{0:T(128)} %param.5) | copy-start | bytes 1540
  43.3 97.3 %all-reduce.5.cloned.1.call-start = ((), (), s32[]{:S(2)}) async-start(), calls=%async_computation.4 | async-start | bytes 131072 | tf_op jit(solution)/shard_map/psum | solution.py:17
  107.3 132.3 %reduce-scatter.6.cloned.1.call-start = ((), (), s32[]{:S(2)}) async-start(), calls=%async_computation.5 | async-start | bytes 1114112 | tf_op jit(solution)/shard_map/reduce_scatter | solution.py:16
  140.6 132.3 %copy-start = (f32[128,128]{1,0:T(8,128)S(1)}, f32[128,128]{1,0:T(8,128)}, u32[]{:S(2)}) copy-start(f32[128,128]{1,0:T(8,128)} %all-reduce.5.cloned.1.call-done) | copy-start | bytes 196612
  174.5 98.5 %all-reduce.7.cloned.1.call-start = ((), (), s32[]{:S(2)}) async-start(), calls=%async_computation.6 | async-start | bytes 131072 | tf_op jit(solution)/shard_map/psum | solution.py:17
  239.6 685.2 %reduce-scatter.8.cloned.1.call-start = ((), (), s32[]{:S(2)}) async-start(), calls=%async_computation.7 | async-start | bytes 1114112 | tf_op jit(solution)/shard_map/reduce_scatter | solution.py:16
  273.8 966.4 %copy-start.1 = (f32[128,128]{1,0:T(8,128)S(1)}, f32[128,128]{1,0:T(8,128)}, u32[]{:S(2)}) copy-start(f32[128,128]{1,0:T(8,128)} %all-reduce.7.cloned.1.call-done) | copy-start | bytes 196612
  864.2 93.9 %all-reduce.9.cloned.1.call-start = ((), (), s32[]{:S(2)}) async-start(), calls=%async_computation.8 | async-start | bytes 131072 | tf_op jit(solution)/shard_map/psum | solution.py:17
Sparse Core Ops, SparseCore 0:
  43.4 63.7 reduce-scatter.3
  109.8 30.8 all-reduce.4
  174.6 64.9 reduce-scatter.5
  242.0 30.9 all-reduce.6
  864.3 60.4 reduce-scatter.7
  927.2 30.8 all-reduce.8
where the time goes:
time: 1250 us
  blocking collectives  918 us (73%)
  waiting for transfers between devices  289 us (23%)
  matrix products  20.2 us (2%)
  between operations  14.1 us (1%)
    psum x2, blocking collectives, squares(): return lax.psum(jnp.sum(residual * residual, axis=0), ('row', 'col'))  557 us
    psum x1, blocking collectives, on_device(): curve_term = lax.psum(jnp.sum(dir_wide * applied, axis=0), ('row', 'col'))  281 us
    reduce_scatter x3, waiting for transfers between devices, apply_models(): lax.psum_scatter(partial_value, 'col', scatter_dimension=0, tiled=True)  189 us
    psum x3, waiting for transfers between devices, apply_models(): return (lax.psum(summed, 'mp'), partial_value)  99.9 us
    all_gather x3, blocking collectives, apply_models(): lax.all_gather(vectors, 'row', axis=1, tiled=True)  80.2 us
  transfers between devices with their start and end apart: 6, of which 6 were waited for; matrix products, arithmetic and copies ran while one was open for 0% of the time, Pallas kernels for 0%

commit v1 on v0

--- a/solution.py
+++ b/solution.py
@@ -36,7 +36,8 @@
         applied, partial_value = apply_models(gram_tile, low_dir[None])
         dir_wide = low_dir.astype(jnp.float32)
         applied = applied + damping[None, :] * dir_wide
-        curve_term = lax.psum(jnp.sum(dir_wide * applied, axis=0), ("row", "col"))
+        local_x = jnp.sum(dir_wide * applied, axis=0)
+        curve_term = lax.psum(lax.psum(local_x, axis_name="row"), axis_name="col")
         step_size = norm_now / curve_term
         merged = merged + step_size[None, :] * direction
         residual = residual - step_size[None, :] * applied

time: 1250 us -> 1060 us (0.85)
  blocking collectives: 918 us -> 721 us
    psum x1 -> x4, blocking collectives: 281 us -> 88.8 us  [on_device(): curve_term = lax.psum(lax.psum(local_x, axis_name='row'), axis_name='col')]
where the time goes in v1:
time: 1060 us; the launch traced here: 1050 us
  blocking collectives  721 us (68%)
  waiting for transfers between devices  290 us (27%)
  matrix products  20.2 us (2%)
  between operations  14.1 us (1%)
    psum x2, blocking collectives, squares(): return lax.psum(jnp.sum(residual * residual, axis=0), ('row', 'col'))  551 us
    reduce_scatter x3, waiting for transfers between devices, apply_models(): lax.psum_scatter(partial_value, 'col', scatter_dimension=0, tiled=True)  190 us
    psum x3, waiting for transfers between devices, apply_models(): return (lax.psum(summed, 'mp'), partial_value)  99.9 us
    psum x4, blocking collectives, on_device(): curve_term = lax.psum(lax.psum(local_x, axis_name='row'), axis_name='col')  88.8 us
    all_gather x3, blocking collectives, apply_models(): lax.all_gather(vectors, 'row', axis=1, tiled=True)  80.2 us
  transfers between devices with their start and end apart: 6, of which 6 were waited for; matrix products, arithmetic and copies ran while one was open for 0% of the time, Pallas kernels for 0%

profile of v1, /device:TPU:4, one launch (start us, length us, event | category | flops | bytes accessed | tf_op | source)
XLA Modules:
  0.0 1051.1 jit_solution(5415844122452989945)
XLA Ops:
  7.2 29.3 %all_gather.9 = bf16[2,1024,128]{2,1,0:T(8,128)(2,1)S(1)} all-gather(bf16[2,128,128]{2,1,0:T(8,128)(2,1)} %param.4), channel_id=1, replica_groups=mesh['mp'=2,'row'=8,'col'=16] {'row'}, dimensions={1}, use_global_device_ids=true | all-gather | bytes 589824 | tf_op jit(solution)/shard_map/all_gather | solution.py:15
  36.5 6.7 convolution_bitcast_fusion.2
  43.3 63.9 %reduce-scatter.4.cloned.1.call-done = f32[128,128]{1,0:T(8,128)} async-done(((f32[2048,128]{1,0:T(8,128)}), f32[128,128]{1,0:T(8,128)}) %reduce-scatter.4.cloned.1.call-update) | async-done | bytes 65552 | tf_op jit(solution)/shard_map/reduce_scatter | solution.py:16
  107.3 33.3 %all-reduce.4.cloned.1.call-done = f32[128,128]{1,0:T(8,128)} async-done(((f32[128,128]{1,0:T(8,128)}), f32[128,128]{1,0:T(8,128)}) %all-reduce.4.cloned.1.call-update) | async-done | bytes 65552 | tf_op jit(solution)/shard_map/psum | solution.py:17
  140.6 0.9 convert_element_type.12
  141.5 26.0 %all-gather = bf16[1024,128]{1,0:T(8,128)(2,1)S(1)} all-gather(bf16[128,128]{1,0:T(8,128)(2,1)S(1)} %convert_element_type.12), channel_id=2, replica_groups=mesh['mp'=2,'row'=8,'col'=16] {'row'}, dimensions={0}, use_global_device_ids=true | all-gather | bytes 294912 | tf_op jit(solution)/shard_map/all_gather | solution.py:15
  167.7 6.7 convolution_bitcast_fusion.1
  174.5 65.0 %reduce-scatter.6.cloned.1.call-done = f32[128,128]{1,0:T(8,128)} async-done(((f32[2048,128]{1,0:T(8,128)}), f32[128,128]{1,0:T(8,128)}) %reduce-scatter.6.cloned.1.call-update) | async-done | bytes 65552 | tf_op jit(solution)/shard_map/reduce_scatter | solution.py:16
  239.6 33.3 %all-reduce.6.cloned.1.call-done = f32[128,128]{1,0:T(8,128)} async-done(((f32[128,128]{1,0:T(8,128)}), f32[128,128]{1,0:T(8,128)}) %all-reduce.6.cloned.1.call-update) | async-done | bytes 65552 | tf_op jit(solution)/shard_map/psum | solution.py:17
  272.9 0.9 fusion.3
  273.8 17.3 %psum.66 = f32[128]{0:T(128)S(1)} all-reduce(f32[128]{0:T(128)S(1)} %get-tuple-element.2), channel_id=1, replica_groups=mesh['mp'=2,'row'=8,'col'=16] {'row'}, use_global_device_ids=true, to_apply=%region_7.0 | all-reduce | flops 128 | bytes 1024 | tf_op jit(solution)/shard_map/psum | solution.py:40
  291.1 27.2 %psum.67 = f32[128]{0:T(128)S(1)} all-reduce(f32[128]{0:T(128)S(1)} %psum.66), channel_id=1, replica_groups=mesh['mp'=2,'row'=8,'col'=16] {'col'}, use_global_device_ids=true, to_apply=%region_8.0 | all-reduce | flops 128 | bytes 1024 | tf_op jit(solution)/shard_map/psum | solution.py:40
  318.3 275.9 %psum.64 = f32[128]{0:T(128)S(1)} all-reduce(f32[128]{0:T(128)S(1)} %get-tuple-element.3), channel_id=1, replica_groups=mesh['mp'=2,'row'=8,'col'=16] {'row','col'}, use_global_device_ids=true, to_apply=%region_3.0 | all-reduce | flops 128 | bytes 1024 | tf_op jit(solution)/shard_map/psum | solution.py:21
  594.2 0.9 multiply_reduce_fusion
  595.1 275.6 %psum.68 = f32[128]{0:T(128)S(1)} all-reduce(f32[128]{0:T(128)S(1)} %multiply_reduce_fusion), channel_id=1, replica_groups=mesh['mp'=2,'row'=8,'col'=16] {'row','col'}, use_global_device_ids=true, to_apply=%region_10.0 | all-reduce | flops 128 | bytes 1024 | tf_op jit(solution)/shard_map/psum | solution.py:21
  870.7 0.9 fusion.6
  871.5 24.9 %all-gather.1 = bf16[1024,128]{1,0:T(8,128)(2,1)S(1)} all-gather(bf16[128,128]{1,0:T(8,128)(2,1)S(1)} %fusion.6), channel_id=3, replica_groups=mesh['mp'=2,'row'=8,'col'=16] {'row'}, dimensions={0}, use_global_device_ids=true | all-gather | bytes 294912 | tf_op jit(solution)/shard_map/all_gather | solution.py:15
  896.6 6.7 convolution_bitcast_fusion
  903.4 60.9 %reduce-scatter.8.cloned.1.call-done = f32[128,128]{1,0:T(8,128)} async-done(((f32[2048,128]{1,0:T(8,128)}), f32[128,128]{1,0:T(8,128)}) %reduce-scatter.8.cloned.1.call-update) | async-done | bytes 65552 | tf_op jit(solution)/shard_map/reduce_scatter | solution.py:16
  964.3 33.2 %all-reduce.8.cloned.1.call-done = f32[128,128]{1,0:T(8,128)} async-done(((f32[128,128]{1,0:T(8,128)}), f32[128,128]{1,0:T(8,128)}) %all-reduce.8.cloned.1.call-update) | async-done | bytes 65552 | tf_op jit(solution)/shard_map/psum | solution.py:17
  997.5 0.9 fusion.5
  998.4 17.2 %psum.70 = f32[128]{0:T(128)S(1)} all-reduce(f32[128]{0:T(128)S(1)} %fusion.5), channel_id=1, replica_groups=mesh['mp'=2,'row'=8,'col'=16] {'row'}, use_global_device_ids=true, to_apply=%region_14.0 | all-reduce | flops 128 | bytes 1024 | tf_op jit(solution)/shard_map/psum | solution.py:40
  1015.6 27.2 %psum.71 = f32[128]{0:T(128)S(1)} all-reduce(f32[128]{0:T(128)S(1)} %psum.70), channel_id=1, replica_groups=mesh['mp'=2,'row'=8,'col'=16] {'col'}, use_global_device_ids=true, to_apply=%region_15.0 | all-reduce | flops 128 | bytes 1024 | tf_op jit(solution)/shard_map/psum | solution.py:40
  1042.8 1.5 multiply_subtract_fusion
  (23 shorter events, 0.7 us)
Async XLA Ops:
  7.2 100.1 %reduce-scatter.4.cloned.1.call-start = ((), (), s32[]{:S(2)}) async-start(), calls=%async_computation.3 | async-start | bytes 1114112 | tf_op jit(solution)/shard_map/reduce_scatter | solution.py:16
  43.3 229.6 %copy-start.2 = (f32[128]{0:T(128)S(1)}, f32[128]{0:T(128)}, u32[]{:S(2)}) copy-start(f32[128]{0:T(128)} %param.5) | copy-start | bytes 1540
  43.3 97.3 %all-reduce.4.cloned.1.call-start = ((), (), s32[]{:S(2)}) async-start(), calls=%async_computation.4 | async-start | bytes 131072 | tf_op jit(solution)/shard_map/psum | solution.py:17
  107.3 132.3 %reduce-scatter.6.cloned.1.call-start = ((), (), s32[]{:S(2)}) async-start(), calls=%async_computation.5 | async-start | bytes 1114112 | tf_op jit(solution)/shard_map/reduce_scatter | solution.py:16
  140.6 132.3 %copy-start = (f32[128,128]{1,0:T(8,128)S(1)}, f32[128,128]{1,0:T(8,128)}, u32[]{:S(2)}) copy-start(f32[128,128]{1,0:T(8,128)} %all-reduce.4.cloned.1.call-done) | copy-start | bytes 196612
  174.5 98.5 %all-reduce.6.cloned.1.call-start = ((), (), s32[]{:S(2)}) async-start(), calls=%async_computation.6 | async-start | bytes 131072 | tf_op jit(solution)/shard_map/psum | solution.py:17
  239.6 724.7 %reduce-scatter.8.cloned.1.call-start = ((), (), s32[]{:S(2)}) async-start(), calls=%async_computation.7 | async-start | bytes 1114112 | tf_op jit(solution)/shard_map/reduce_scatter | solution.py:16
  273.8 769.0 %copy-start.1 = (f32[128,128]{1,0:T(8,128)S(1)}, f32[128,128]{1,0:T(8,128)}, u32[]{:S(2)}) copy-start(f32[128,128]{1,0:T(8,128)} %all-reduce.6.cloned.1.call-done) | copy-start | bytes 196612
  903.3 94.2 %all-reduce.8.cloned.1.call-start = ((), (), s32[]{:S(2)}) async-start(), calls=%async_computation.8 | async-start | bytes 131072 | tf_op jit(solution)/shard_map/psum | solution.py:17
Sparse Core Ops, SparseCore 0:
  43.4 63.7 reduce-scatter.3
  109.8 30.8 all-reduce.3
  174.6 64.9 reduce-scatter.5
  242.0 30.9 all-reduce.5
  903.4 60.7 reduce-scatter.7
  966.7 30.8 all-reduce.7
